TPU v7x, 32 devices: a whole 2x2x4 slice. The times are simulated.
32 devices in a mesh: row: 8 (over y, x, core), col: 4 (over z).
Axes of the slice: x: 2, y: 2, z: 4, core: 2. Of those that a mesh axis runs over, the one named last changes fastest.
Arguments:
- matrix: bfloat16 [3072, 3072], P('row', 'col'), may hold values from 3.2484531e-06 to 0.0012969971
- occ_matrix: int32 [24, 24], P('row', 'col'), may hold values 0 or 1
- batch: bfloat16 [3072, 512], P('row', 'col'), may hold values from 0.0099487305 to 4
- occ_batch: int32 [24, 4], P('row', 'col'), may hold values 0 or 1
- prune_mask: int32 [3072, 512], P('row', 'col'), may hold values 0 or 1
Outputs:
- clustered: float32 [3072, 512], P('row', 'col')
All inputs are finite; a program needn't handle non-finite values. No bound on the sum of `occ_matrix` or of `occ_batch` or of `prune_mask` on one device may be relied on, other than what follows from the above.
Results may differ from a plain program's by a relative error of at most 0.0003.
Values may be sent and summed in bfloat16 or wider, within the bound.
A program may use at most 64 MiB of HBM per device.

v0:
```python
import jax
import jax.numpy as jnp
from jax import lax
from jax.sharding import PartitionSpec as P


def expand_tiles(occupancy, size):
    return jnp.repeat(jnp.repeat(occupancy, size, axis=0), size, axis=1)


def body(matrix, occ_matrix, batch, occ_batch, prune_mask):
    tile_size = matrix.shape[0] // occ_matrix.shape[0]
    stored_matrix = matrix * expand_tiles(occ_matrix, tile_size).astype(jnp.bfloat16)
    stored_batch = batch * expand_tiles(occ_batch, tile_size).astype(jnp.bfloat16)
    whole_batch = lax.all_gather(stored_batch, "row", axis=0, tiled=True)
    expanded = jnp.dot(
        lax.all_gather(stored_matrix, "col", axis=1, tiled=True),
        whole_batch,
        preferred_element_type=jnp.float32,
    )
    kept = expanded * prune_mask.astype(jnp.float32)
    inflated = kept * kept
    col_total = lax.psum(jnp.sum(inflated, axis=0), "row")
    order = matrix.shape[0] * lax.axis_size("row")
    return inflated / (col_total[None, :] / order + 1e-05)


def solution(mesh):
    placed = (P("row", "col"), P("row", "col"), P("row", "col"), P("row", "col"), P("row", "col"))
    return jax.shard_map(
        body, mesh=mesh, in_specs=placed, out_specs=P("row", "col"), check_vma=False
    )
```

profile of v0, /device:TPU:0, one launch (start us, length us, event | category | flops | bytes accessed | tf_op | source)
XLA Modules:
  0.0 86.1 jit_solution(16578038678067250543)
XLA Ops:
  6.5 0.0 copy-start.2
  6.5 0.0 copy-start.1
  6.5 0.0 copy-start
  6.5 0.0 all-gather.2.cloned.1.call-start
  6.5 0.7 convert_element_type.25
  7.3 0.1 copy.6
  7.4 0.1 broadcast_bitcast_fusion
  7.5 1.4 %copy.7 = bf16[384,768]{0,1:T(8,128)(2,1)S(1)} copy(bf16[384,768]{1,0:T(8,128)(2,1)} %param.5) | data formatting | bytes 1179648 | tf_op args[0]
  8.8 0.9 %bitcast_multiply_fusion = bf16[384,768]{0,1:T(8,128)(2,1)} fusion(bf16[384,768]{0,1:T(8,128)(2,1)S(1)} %copy.7, bf16[384,6]{0,1:T(8,128)(2,1)S(1)} %bitcast.15), kind=kLoop, calls=%fused_computation.2 | loop fusion | flops 294912 | bytes 1184256 | tf_op jit(solution)/shard_map/mul | solution.py:13
  9.7 0.0 all-gather.2.cloned.1.call-update
  9.7 0.0 copy-done.2
  9.8 0.1 broadcast_bitcast_fusion.1
  9.8 0.0 copy-done.1
  9.8 0.1 broadcast_multiply_fusion
  10.0 11.9 %all_gather.7 = bf16[3072,128]{1,0:T(8,128)(2,1)S(1)} all-gather(bf16[384,128]{1,0:T(8,128)(2,1)S(1)} %broadcast_multiply_fusion), channel_id=1, replica_groups=mesh['row'=8,'col'=4] {'row'}, dimensions={0}, use_global_device_ids=true | all-gather | bytes 884736 | tf_op jit(solution)/shard_map/all_gather | solution.py:15
  21.8 40.8 %all-gather.2.cloned.1.call-done = bf16[384,3072]{0,1:T(8,128)(2,1)} async-done(((bf16[384,768]{0,1:T(8,128)(2,1)}), bf16[384,3072]{0,1:T(8,128)(2,1)}) %all-gather.2.cloned.1.call-update) | async-done | bytes 2359312 | tf_op jit(solution)/shard_map/all_gather | solution.py:17
  62.6 0.0 copy-done
  62.6 2.5 %fusion.1 = (f32[128]{0:T(128)S(1)}, f32[384,128]{1,0:T(8,128)S(1)}) fusion(s32[384,128]{1,0:T(8,128)S(1)} %copy-done, bf16[384,3072]{0,1:T(8,128)(2,1)} %all-gather.2.cloned.1.call-done, bf16[3072,128]{1,0:T(8,128)(2,1)S(1)} %all_gather.7), kind=kOutput, calls=%fused_computation.10 | convolution fusion | flops 302186368 | bytes 3539456 | tf_op jit(solution)/shard_map/dot_general | solution.py:16
  65.1 13.4 %psum.7 = f32[128]{0:T(128)S(1)} all-reduce(f32[128]{0:T(128)S(1)} %get-tuple-element.5), channel_id=1, replica_groups=mesh['row'=8,'col'=4] {'row'}, use_global_device_ids=true, to_apply=%region_1.0 | all-reduce | flops 128 | bytes 1024 | tf_op jit(solution)/shard_map/psum | solution.py:23
  78.5 0.7 broadcast_divide_fusion
  (3 shorter events, 0.0 us)
Async XLA Ops:
  6.5 3.2 %copy-start.2 = (s32[3,1]{0,1:T(1,128)S(1)}, s32[3,1]{0,1:T(1,128)}, u32[]{:S(2)}) copy-start(s32[3,1]{0,1:T(1,128)} %param.8) | copy-start | bytes 40
  6.5 3.3 %copy-start.1 = (bf16[384,128]{1,0:T(8,128)(2,1)S(1)}, bf16[384,128]{1,0:T(8,128)(2,1)}, u32[]{:S(2)}) copy-start(bf16[384,128]{1,0:T(8,128)(2,1)} %param.7) | copy-start | bytes 294916
  6.5 56.1 %copy-start = (s32[384,128]{1,0:T(8,128)S(1)}, s32[384,128]{1,0:T(8,128)}, u32[]{:S(2)}) copy-start(s32[384,128]{1,0:T(8,128)} %param.9) | copy-start | bytes 589828
  6.5 56.1 %all-gather.2.cloned.1.call-start = ((), (), s32[]{:S(2)}) async-start(), calls=%async_computation | async-start | bytes 2949120 | tf_op jit(solution)/shard_map/all_gather | solution.py:17
Sparse Core Ops, SparseCore 0:
  9.9 52.6 all-gather.1
where the time goes:
time: 86.3 us; the launch traced here: 86.1 us
  waiting for transfers between devices  40.8 us (47%)
  blocking collectives  25.3 us (29%)
  between operations  13.4 us (16%)
  matrix products  2.49 us (3%)
  other arithmetic  2.44 us (3%)
  local copies, waits for them, and re-layouts  1.64 us (2%)
    all_gather x1, waiting for transfers between devices, body(): lax.all_gather(stored_matrix, 'col', axis=1, tiled=True)  40.8 us
    psum x1, blocking collectives, body(): col_total = lax.psum(jnp.sum(inflated, axis=0), 'row')  13.4 us
    all_gather x1, blocking collectives, body(): whole_batch = lax.all_gather(stored_batch, 'row', axis=0, tiled=True)  11.9 us
    dot_general x1, matrix products, body(): jnp.dot(lax.all_gather(stored_matrix, 'col', axis=1, tiled=True), whole_b...  2.49 us
  transfers between devices with their start and end apart: 1, of which 1 were waited for; matrix products, arithmetic and copies ran while one was open for 0% of the time, Pallas kernels for 0%

commit v1 on v0

v1 whole, which is shorter than its diff:
```python
import functools

import jax
import jax.numpy as jnp
from jax import lax
from jax.experimental import pallas as pl
from jax.experimental.pallas import tpu as pltpu
from jax.sharding import PartitionSpec as P

MESH = pl.DeviceIdType.MESH


def expand_tiles(occupancy, size):
    return jnp.repeat(jnp.repeat(occupancy, size, axis=0), size, axis=1)


def plain_body(matrix, occ_matrix, batch, occ_batch, prune_mask):
    tile_size = matrix.shape[0] // occ_matrix.shape[0]
    stored_matrix = matrix * expand_tiles(occ_matrix, tile_size).astype(jnp.bfloat16)
    stored_batch = batch * expand_tiles(occ_batch, tile_size).astype(jnp.bfloat16)
    whole_batch = lax.all_gather(stored_batch, "row", axis=0, tiled=True)
    expanded = jnp.dot(
        lax.all_gather(stored_matrix, "col", axis=1, tiled=True),
        whole_batch,
        preferred_element_type=jnp.float32,
    )
    kept = expanded * prune_mask.astype(jnp.float32)
    inflated = kept * kept
    col_total = lax.psum(jnp.sum(inflated, axis=0), "row")
    order = matrix.shape[0] * lax.axis_size("row")
    return inflated / (col_total[None, :] / order + 1e-05)


def kernel(
    R, C, mat_hbm, occ_m, bat, occ_b, prune_hbm, infl_out, tot_out,
    a_buf, prune_buf, sb, bk, acc, up, down, tots,
    load_sems, s1, r1, s2, r2, f2, us, ur, ds, dr, ts, tr,
):
    rho = R // C
    rows, depth = a_buf.shape
    piece = rows // C
    tile = rows // occ_m.shape[0]
    chunk = tile
    J = rows // chunk
    r, c = lax.axis_index("row"), lax.axis_index("col")
    p, e = lax.div(r, rho), lax.rem(r, rho)

    def remote(src, dst, ssem, rsem, row, col):
        return pltpu.make_async_remote_copy(
            src_ref=src, dst_ref=dst, send_sem=ssem, recv_sem=rsem,
            device_id={"row": row, "col": col}, device_id_type=MESH,
        )

    barrier = pltpu.get_barrier_semaphore()

    def greet(row, col):
        pl.semaphore_signal(
            barrier, inc=1, device_id={"row": row, "col": col}, device_id_type=MESH
        )

    for k in range(1, C):
        greet(c * rho + e, lax.rem(c + k, C))
    for k in range(1, R):
        greet(lax.rem(r + k, R), c)

    @pl.when(c > 0)
    def _():
        greet(r, c - 1)

    @pl.when(c < C - 1)
    def _():
        greet(r, c + 1)

    load_a = pltpu.make_async_copy(mat_hbm, a_buf, load_sems.at[0])
    load_a.start()
    load_prune = pltpu.make_async_copy(prune_hbm, prune_buf, load_sems.at[1])
    load_prune.start()
    for t in range(rows // tile):
        part = pl.ds(t * tile, tile)
        sb[part, :] = bat[part, :] * occ_b[t, 0].astype(jnp.float32).astype(jnp.bfloat16)

    greeted = (
        R - 1
        + jnp.where(c > 0, 1, 0)
        + jnp.where(c < C - 1, 1, 0)
        + jnp.where(c != p, C, 0)
    )
    pl.semaphore_wait(barrier, greeted)

    def scatter(q):
        return remote(
            sb.at[pl.ds(q * piece, piece)], bk.at[e, q, c],
            s1.at[q], r1.at[c], q * rho + e, p,
        )

    for q in range(C):
        own = jnp.logical_and(p == q, c == p)

        @pl.when(own)
        def _():
            pltpu.make_async_copy(
                sb.at[pl.ds(q * piece, piece)], bk.at[e, q, c], r1.at[c]
            ).start()

        @pl.when(jnp.logical_not(own))
        def _():
            scatter(q).start()

    load_a.wait()
    for i in range(rows // tile):
        for j in range(depth // tile):
            at = (pl.ds(i * tile, tile), pl.ds(j * tile, tile))
            a_buf[at] = a_buf[at] * occ_m[i, j].astype(jnp.float32).astype(jnp.bfloat16)

    for j in range(C):
        got = bk.at[e, p, j]
        remote(got, got, s1.at[0], r1.at[j], r, c).wait_recv()

    sends = []
    for k in range(1, C):
        copy = remote(
            bk.at[e, p], bk.at[e, p], s2.at[k - 1], r2.at[e, p],
            lax.rem(p + k, C) * rho + e, c,
        )
        copy.start()
        sends.append(copy)
    for k in range(C):
        q = lax.rem(p + k, C)
        if k:
            got = bk.at[e, q]
            remote(got, got, s2.at[0], r2.at[e, q], r, c).wait_recv()
        for d in range(1, rho):
            copy = remote(
                bk.at[e, q], bk.at[e, q], f2.at[d - 1, k], r2.at[e, q],
                p * rho + lax.rem(e + d, rho), c,
            )
            copy.start()
            sends.append(copy)
    for d in range(1, rho):
        for k in range(C):
            q = lax.rem(p + k, C)
            other = lax.rem(e + d, rho)
            got = bk.at[other, q]
            remote(got, got, s2.at[0], r2.at[other, q], r, c).wait_recv()

    for i in range(C // 2 + C % 2):
        for b in sorted({C - 1 - i, i}, reverse=True):
            rhs = bk[:, :, b].reshape(depth, bk.shape[-1])
            acc[b] = jnp.dot(a_buf[...], rhs, preferred_element_type=jnp.float32)

    def up_copy(b, j):
        part = pl.ds(j * chunk, chunk)
        return remote(
            acc.at[b, part], up.at[b, part], us.at[b, j], ur.at[b, j], r, c + 1
        )

    def down_copy(b, j):
        part = pl.ds(j * chunk, chunk)
        return remote(
            acc.at[b, part], down.at[b, part], ds.at[b, j], dr.at[b, j], r, c - 1
        )

    def take(buf, sems, b, j):
        part = pl.ds(j * chunk, chunk)
        got = buf.at[b, part]
        remote(got, got, us.at[0, 0], sems.at[b, j], r, c).wait_recv()
        acc[b, part] = acc[b, part] + buf[b, part]

    for i in range(C - 1):
        for j in range(J):
            b = C - 1 - i

            @pl.when(c < b)
            def _():
                @pl.when(c > 0)
                def _():
                    take(up, ur, b, j)

                up_copy(b, j).start()

            @pl.when(c > i)
            def _():
                @pl.when(c < C - 1)
                def _():
                    take(down, dr, i, j)

                down_copy(i, j).start()

    load_prune.wait()
    for j in range(J):
        @pl.when(c > 0)
        def _():
            take(up, ur, c, j)

        @pl.when(c < C - 1)
        def _():
            take(down, dr, c, j)

    kept = acc[c] * prune_buf[...].astype(jnp.float32)
    inflated = kept * kept
    infl_out[...] = inflated
    tots[r] = jnp.broadcast_to(
        jnp.sum(inflated, axis=0, keepdims=True), tots.shape[1:]
    )
    for k in range(1, R):
        copy = remote(
            tots.at[r], tots.at[r], ts.at[k - 1], tr.at[r], lax.rem(r + k, R), c
        )
        copy.start()
        sends.append(copy)
    for k in range(1, R):
        other = lax.rem(r + k, R)
        got = tots.at[other]
        remote(got, got, ts.at[0], tr.at[other], r, c).wait_recv()
    total = tots[0]
    for k in range(1, R):
        total = total + tots[k]
    tot_out[...] = total

    for copy in sends:
        copy.wait_send()
    for q in range(C):
        @pl.when(jnp.logical_not(jnp.logical_and(p == q, c == p)))
        def _():
            scatter(q).wait_send()
    for i in range(C - 1):
        for j in range(J):
            b = C - 1 - i

            @pl.when(c < b)
            def _():
                up_copy(b, j).wait_send()

            @pl.when(c > i)
            def _():
                down_copy(i, j).wait_send()


def kernel_body(R, C, matrix, occ_matrix, batch, occ_batch, prune_mask):
    rho = R // C
    rows, depth = matrix.shape
    cols = batch.shape[1]
    J = rows // (rows // occ_matrix.shape[0])
    vmem, smem, hbm = (pl.BlockSpec(memory_space=s) for s in (pltpu.VMEM, pltpu.SMEM, pl.ANY))
    dma = pltpu.SemaphoreType.DMA
    f32, bf16 = jnp.float32, jnp.bfloat16
    inflated, total = pl.pallas_call(
        functools.partial(kernel, R, C),
        out_shape=(
            jax.ShapeDtypeStruct((rows, cols), f32),
            jax.ShapeDtypeStruct((8, cols), f32),
        ),
        in_specs=[hbm, smem, vmem, smem, hbm],
        out_specs=(vmem, vmem),
        scratch_shapes=[
            pltpu.VMEM((rows, depth), bf16),
            pltpu.VMEM((rows, cols), jnp.int32),
            pltpu.VMEM((rows, cols), bf16),
            pltpu.VMEM((rho, C, C, rows // C, cols), bf16),
            pltpu.VMEM((C, rows, cols), f32),
            pltpu.VMEM((C, rows, cols), f32),
            pltpu.VMEM((C, rows, cols), f32),
            pltpu.VMEM((R, 8, cols), f32),
            dma((2,)),
            dma((C,)),
            dma((C,)),
            dma((C - 1,)),
            dma((rho, C)),
            dma((max(rho - 1, 1), C)),
            dma((C, J)),
            dma((C, J)),
            dma((C, J)),
            dma((C, J)),
            dma((R - 1,)),
            dma((R,)),
        ],
        compiler_params=pltpu.CompilerParams(collective_id=0, has_side_effects=True),
    )(matrix, occ_matrix, batch, occ_batch, prune_mask)
    return inflated / (total[:1] / (rows * R) + 1e-05)


def body(R, C, matrix, occ_matrix, batch, occ_batch, prune_mask):
    rows = matrix.shape[0]
    fits = (
        1 < C <= 8 and R % C == 0 and R <= 16
        and rows % (16 * C) == 0 and matrix.shape[1] == rows * (R // C)
    )
    chosen = functools.partial(kernel_body, R, C) if fits else plain_body
    return chosen(matrix, occ_matrix, batch, occ_batch, prune_mask)


def solution(mesh):
    R, C = mesh.shape["row"], mesh.shape["col"]
    placed = (P("row", "col"),) * 5
    return jax.shard_map(
        functools.partial(body, R, C), mesh=mesh, in_specs=placed,
        out_specs=P("row", "col"), check_vma=False,
    )
```

time: 86.3 us -> 56.1 us (0.65)
  Pallas kernels: 0 us -> 52.3 us
  waiting for transfers between devices: 40.8 us -> 0 us
  blocking collectives: 25.3 us -> 0 us
  between operations: 13.4 us -> 0.01 us
  matrix products: 2.49 us -> 0 us
    pallas_call x0 -> x1, Pallas kernels: none -> 52.3 us  [kernel_body(): pl.pallas_call(functools.partial(kernel, R, C), out_shape=(jax.ShapeDtype...]
    all_gather x1 -> x0, waiting for transfers between devices: 40.8 us -> none  [body(): lax.all_gather(stored_matrix, 'col', axis=1, tiled=True)]
    psum x1 -> x0, blocking collectives: 13.4 us -> none  [body(): col_total = lax.psum(jnp.sum(inflated, axis=0), 'row')]
    all_gather x1 -> x0, blocking collectives: 11.9 us -> none  [body(): whole_batch = lax.all_gather(stored_batch, 'row', axis=0, tiled=True)]
    dot_general x1 -> x0, matrix products: 2.49 us -> none  [body(): jnp.dot(lax.all_gather(stored_matrix, 'col', axis=1, tiled=True), whole_b...]
    div x1 -> x2, other arithmetic: 0.7 us -> 2.3 us  [kernel_body(): return inflated / (total[:1] / (rows * R) + 1e-05)]
    mul x2 -> x0, other arithmetic: 0.99 us -> none  [the longest x1 0.88 us: body(): matrix * expand_tiles(occ_matrix, tile_size).astype(jnp.bfloat16)]
  transfers between devices with their start and end apart: 1 -> 0, of which waited for: 1 -> 0; matrix products, arithmetic and copies ran while one was open for 0% -> 0% of each run, Pallas kernels for 0% -> 0%
where the time goes in v1:
time: 56.1 us; the launch traced here: 55.9 us
  Pallas kernels  52.3 us (93%)
  other arithmetic  2.3 us (4%)
  local copies, waits for them, and re-layouts  1.31 us (2%)
    pallas_call x1, Pallas kernels, kernel_body(): pl.pallas_call(functools.partial(kernel, R, C), out_shape=(jax.ShapeDtype...  52.3 us
    div x2, other arithmetic, kernel_body(): return inflated / (total[:1] / (rows * R) + 1e-05)  2.3 us
    unnamed x1, local copies, waits for them, and re-layouts  1.31 us

profile of v1, /device:TPU:0, one launch (start us, length us, event | category | flops | bytes accessed | tf_op | source)
XLA Modules:
  0.0 55.9 jit_solution(8251385751657963164)
XLA Ops:
  0.0 1.3 %copy.6.occ_b = s32[3,1]{1,0:T(4,128)} copy(s32[3,1]{0,1:T(1,128)} %param.8) | data formatting | bytes 24 | tf_op args[3]
  1.3 52.3 %shard_map.55 = (f32[384,128]{1,0:T(8,128)}, f32[8,128]{1,0:T(8,128)}) custom-call(bf16[384,768]{1,0:T(8,128)(2,1)} %mat_hbm.1, s32[3,6]{1,0:T(4,128)} %occ_m.1, bf16[384,128]{1,0:T(8,128)(2,1)} %bat.1, s32[3,1]{1,0:T(4,128)} %copy.6.occ_b, s32[384,128]{1,0:T(8,128)} %prune_hbm.1), custom_call_target="tpu_custom_call" | custom-call | tf_op jit(solution)/shard_map/pallas_call | solution.py:247
  53.6 0.7 %add_bitcast_fusion = f32[128]{0:T(128)S(1)} fusion(f32[8,128]{1,0:T(8,128)} %get-tuple-element.8), kind=kLoop, calls=%fused_computation.1 | loop fusion | flops 256 | bytes 1024 | tf_op jit(solution)/shard_map/div | solution.py:279
  54.3 1.6 %broadcast_divide_fusion = f32[384,128]{1,0:T(8,128)} fusion(f32[384,128]{1,0:T(8,128)} %get-tuple-element.7, f32[128]{0:T(128)S(1)} %add_bitcast_fusion), kind=kLoop, calls=%fused_computation | loop fusion | flops 49152 | bytes 393728 | tf_op jit(solution)/shard_map/div | solution.py:279

commit v2 on v1

v2 whole, which is shorter than its diff:
```python
import functools

import jax
import jax.numpy as jnp
from jax import lax
from jax.experimental import pallas as pl
from jax.experimental.pallas import tpu as pltpu
from jax.sharding import PartitionSpec as P

MESH = pl.DeviceIdType.MESH

LOWEST = -24.0
STEPS = 2047.0
LN2 = 0.6931471805599453


def encode(x):
    safe = jnp.maximum(x, 2.0**LOWEST)
    level = jnp.minimum((jnp.log(safe) * (1.0 / LN2) - LOWEST) * STEPS, 65533.0) + 1.5
    code = jnp.where(x > 0, level.astype(jnp.int32), 0)
    return (code - 32768).astype(jnp.int16)


def decode(code):
    level = code.astype(jnp.int32) + 32767
    value = jnp.exp((level.astype(jnp.float32) * (1.0 / STEPS) + LOWEST) * LN2)
    return jnp.where(level >= 0, value, 0.0)


def expand_tiles(occupancy, size):
    return jnp.repeat(jnp.repeat(occupancy, size, axis=0), size, axis=1)


def plain_body(matrix, occ_matrix, batch, occ_batch, prune_mask):
    tile_size = matrix.shape[0] // occ_matrix.shape[0]
    stored_matrix = matrix * expand_tiles(occ_matrix, tile_size).astype(jnp.bfloat16)
    stored_batch = batch * expand_tiles(occ_batch, tile_size).astype(jnp.bfloat16)
    whole_batch = lax.all_gather(stored_batch, "row", axis=0, tiled=True)
    expanded = jnp.dot(
        lax.all_gather(stored_matrix, "col", axis=1, tiled=True),
        whole_batch,
        preferred_element_type=jnp.float32,
    )
    kept = expanded * prune_mask.astype(jnp.float32)
    inflated = kept * kept
    col_total = lax.psum(jnp.sum(inflated, axis=0), "row")
    order = matrix.shape[0] * lax.axis_size("row")
    return inflated / (col_total[None, :] / order + 1e-05)


def kernel(
    R, C, mat_hbm, occ_m, bat, occ_b, prune_hbm, infl_out, tot_out,
    a_buf, prune_buf, sb, bk, own, out_buf, in_buf, tots,
    load_sems, s1, r1, s2, r2, f2, zs, zr, ts, tr,
):
    rho = R // C
    rows, depth = a_buf.shape
    piece = rows // C
    tile = rows // occ_m.shape[0]
    r, c = lax.axis_index("row"), lax.axis_index("col")
    p, e = lax.div(r, rho), lax.rem(r, rho)

    def remote(src, dst, ssem, rsem, row, col):
        return pltpu.make_async_remote_copy(
            src_ref=src, dst_ref=dst, send_sem=ssem, recv_sem=rsem,
            device_id={"row": row, "col": col}, device_id_type=MESH,
        )

    barrier = pltpu.get_barrier_semaphore()

    def greet(row, col):
        pl.semaphore_signal(
            barrier, inc=1, device_id={"row": row, "col": col}, device_id_type=MESH
        )

    for k in range(1, C):
        greet(c * rho + e, lax.rem(c + k, C))
    for k in range(1, R):
        greet(lax.rem(r + k, R), c)

    for k in range(1, C):
        greet(r, lax.rem(c + k, C))

    load_a = pltpu.make_async_copy(mat_hbm, a_buf, load_sems.at[0])
    load_a.start()
    load_prune = pltpu.make_async_copy(prune_hbm, prune_buf, load_sems.at[1])
    load_prune.start()
    for t in range(rows // tile):
        part = pl.ds(t * tile, tile)
        sb[part, :] = bat[part, :] * occ_b[t].astype(jnp.float32).astype(jnp.bfloat16)

    greeted = R - 1 + C - 1 + jnp.where(c != p, C, 0)
    pl.semaphore_wait(barrier, greeted)

    def scatter(q):
        return remote(
            sb.at[pl.ds(q * piece, piece)], bk.at[e, q, c],
            s1.at[q], r1.at[c], q * rho + e, p,
        )

    for q in range(C):
        stays = jnp.logical_and(p == q, c == p)

        @pl.when(stays)
        def _():
            pltpu.make_async_copy(
                sb.at[pl.ds(q * piece, piece)], bk.at[e, q, c], r1.at[c]
            ).start()

        @pl.when(jnp.logical_not(stays))
        def _():
            scatter(q).start()

    load_a.wait()
    for i in range(rows // tile):
        for j in range(depth // tile):
            at = (pl.ds(i * tile, tile), pl.ds(j * tile, tile))
            a_buf[at] = a_buf[at] * occ_m[i, j].astype(jnp.float32).astype(jnp.bfloat16)

    sends = []
    order = [lax.rem(c + k, C) for k in list(range(1, C)) + [0]]

    def send(src, ssem, rsem, row):
        copy = remote(src, src, ssem, rsem, row, c)
        copy.start()
        sends.append(copy)

    def arrived(ref, rsem):
        remote(ref, ref, s1.at[0], rsem, r, c).wait_recv()

    for n, b in enumerate(order):
        mine = bk.at[e, p, b]
        arrived(mine, r1.at[b])
        for k in range(1, C):
            send(mine, s2.at[n, k], r2.at[e, p, b], lax.rem(p + k, C) * rho + e)
        for d in range(1, rho):
            send(mine, f2.at[n, d, 0], r2.at[e, p, b], p * rho + lax.rem(e + d, rho))

    for n, b in enumerate(order):
        for k in range(1, C):
            q = lax.rem(p + k, C)
            got = bk.at[e, q, b]
            arrived(got, r2.at[e, q, b])
            for d in range(1, rho):
                send(got, f2.at[n, d, k], r2.at[e, q, b], p * rho + lax.rem(e + d, rho))
        for d in range(1, rho):
            other = lax.rem(e + d, rho)
            for k in range(C):
                q = lax.rem(p + k, C)
                arrived(bk.at[other, q, b], r2.at[other, q, b])
        rhs = bk[:, :, b].reshape(depth, bk.shape[-1])
        part = jnp.dot(a_buf[...], rhs, preferred_element_type=jnp.float32)
        if n < C - 1:
            out_buf[n] = encode(part)
            copy = remote(out_buf.at[n], in_buf.at[C - 2 - n], zs.at[n], zr.at[C - 2 - n], r, b)
            copy.start()
            sends.append(copy)
        else:
            own[...] = part

    load_prune.wait()
    for n in range(C - 1):
        slot = in_buf.at[n]
        remote(slot, slot, zs.at[n], zr.at[n], r, c).wait_recv()
        own[...] = own[...] + decode(in_buf[n])

    kept = own[...] * prune_buf[...].astype(jnp.float32)
    inflated = kept * kept
    infl_out[...] = inflated
    tots[r] = jnp.broadcast_to(
        jnp.sum(inflated, axis=0, keepdims=True), tots.shape[1:]
    )
    for k in range(1, R):
        copy = remote(
            tots.at[r], tots.at[r], ts.at[k - 1], tr.at[r], lax.rem(r + k, R), c
        )
        copy.start()
        sends.append(copy)
    for k in range(1, R):
        other = lax.rem(r + k, R)
        got = tots.at[other]
        remote(got, got, ts.at[0], tr.at[other], r, c).wait_recv()
    total = tots[0]
    for k in range(1, R):
        total = total + tots[k]
    tot_out[...] = total / (rows * R) + 1e-05

    for copy in sends:
        copy.wait_send()
    for q in range(C):
        @pl.when(jnp.logical_not(jnp.logical_and(p == q, c == p)))
        def _():
            scatter(q).wait_send()


def kernel_body(R, C, matrix, occ_matrix, batch, occ_batch, prune_mask):
    rho = R // C
    rows, depth = matrix.shape
    cols = batch.shape[1]
    vmem, smem, hbm = (pl.BlockSpec(memory_space=s) for s in (pltpu.VMEM, pltpu.SMEM, pl.ANY))
    dma = pltpu.SemaphoreType.DMA
    f32, bf16 = jnp.float32, jnp.bfloat16
    inflated, total = pl.pallas_call(
        functools.partial(kernel, R, C),
        out_shape=(
            jax.ShapeDtypeStruct((rows, cols), f32),
            jax.ShapeDtypeStruct((1, cols), f32),
        ),
        in_specs=[hbm, smem, vmem, smem, hbm],
        out_specs=(vmem, vmem),
        scratch_shapes=[
            pltpu.VMEM((rows, depth), bf16),
            pltpu.VMEM((rows, cols), jnp.int32),
            pltpu.VMEM((rows, cols), bf16),
            pltpu.VMEM((rho, C, C, rows // C, cols), bf16),
            pltpu.VMEM((rows, cols), f32),
            pltpu.VMEM((C - 1, rows, cols), jnp.int16),
            pltpu.VMEM((C - 1, rows, cols), jnp.int16),
            pltpu.VMEM((R, 1, cols), f32),
            dma((2,)),
            dma((C,)),
            dma((C,)),
            dma((C, C)),
            dma((rho, C, C)),
            dma((C, rho, C)),
            dma((C - 1,)),
            dma((C - 1,)),
            dma((R - 1,)),
            dma((R,)),
        ],
        compiler_params=pltpu.CompilerParams(collective_id=0, has_side_effects=True),
    )(matrix, occ_matrix, batch, occ_batch[:, 0], prune_mask)
    return inflated / total


def body(R, C, matrix, occ_matrix, batch, occ_batch, prune_mask):
    rows = matrix.shape[0]
    fits = (
        1 < C <= 8 and R % C == 0 and R <= 16
        and rows % (16 * C) == 0 and matrix.shape[1] == rows * (R // C)
    )
    chosen = functools.partial(kernel_body, R, C) if fits else plain_body
    return chosen(matrix, occ_matrix, batch, occ_batch, prune_mask)


def solution(mesh):
    R, C = mesh.shape["row"], mesh.shape["col"]
    placed = (P("row", "col"),) * 5
    return jax.shard_map(
        functools.partial(body, R, C), mesh=mesh, in_specs=placed,
        out_specs=P("row", "col"), check_vma=False,
    )
```

time: 56.1 us -> 33.1 us (0.59)
  Pallas kernels: 52.3 us -> 30.7 us
  local copies, waits for them, and re-layouts: 1.31 us -> 0.6 us
  other arithmetic: 2.3 us -> 1.62 us
    pallas_call x1, Pallas kernels: 52.3 us -> 30.7 us  [kernel_body(): pl.pallas_call(functools.partial(kernel, R, C), out_shape=(jax.ShapeDtype...]
    unnamed x1 -> x2, local copies, waits for them, and re-layouts: 1.31 us -> 0.6 us
    div x2 -> x1, other arithmetic: 2.3 us -> 1.62 us  [kernel_body(): return inflated / total]
where the time goes in v2:
time: 33.1 us; the launch traced here: 32.9 us
  Pallas kernels  30.7 us (93%)
  other arithmetic  1.62 us (5%)
  local copies, waits for them, and re-layouts  0.6 us (2%)
    pallas_call x1, Pallas kernels, kernel_body(): pl.pallas_call(functools.partial(kernel, R, C), out_shape=(jax.ShapeDtype...  30.7 us
    div x1, other arithmetic, kernel_body(): return inflated / total  1.62 us

profile of v2, /device:TPU:0, one launch (start us, length us, event | category | flops | bytes accessed | tf_op | source)
XLA Modules:
  0.0 32.9 jit_solution(2924456762835363871)
XLA Ops:
  0.0 30.7 %shard_map.55 = (f32[384,128]{1,0:T(8,128)}, f32[1,128]{1,0:T(1,128)}) custom-call(bf16[384,768]{1,0:T(8,128)(2,1)} %mat_hbm.1, s32[3,6]{1,0:T(4,128)} %occ_m.1, bf16[384,128]{1,0:T(8,128)(2,1)} %bat.1, s32[3]{0:T(128)} %bitcast.2, s32[384,128]{1,0:T(8,128)} %prune_hbm.1), custom_call_target="tpu_custom_call" | custom-call | tf_op jit(solution)/shard_map/pallas_call | solution.py:203
  30.7 0.0 copy-start
  30.7 0.6 %copy-done = f32[1,128]{1,0:T(1,128)S(1)} copy-done((f32[1,128]{1,0:T(1,128)S(1)}, f32[1,128]{1,0:T(1,128)}, u32[]{:S(2)}) %copy-start) | copy-done | bytes 536
  31.3 1.6 %broadcast_divide_fusion = f32[384,128]{1,0:T(8,128)} fusion(f32[384,128]{1,0:T(8,128)} %get-tuple-element.7, f32[128]{0:T(128)S(1)} %bitcast.3), kind=kLoop, calls=%fused_computation | loop fusion | flops 49152 | bytes 393728 | tf_op jit(solution)/shard_map/div | solution.py:233
Async XLA Ops:
  30.7 0.6 %copy-start = (f32[1,128]{1,0:T(1,128)S(1)}, f32[1,128]{1,0:T(1,128)}, u32[]{:S(2)}) copy-start(f32[1,128]{1,0:T(1,128)} %get-tuple-element.8) | copy-start | bytes 1540

commit v3 on v2

--- a/solution.py
+++ b/solution.py
@@ -118,7 +118,14 @@
             a_buf[at] = a_buf[at] * occ_m[i, j].astype(jnp.float32).astype(jnp.bfloat16)
 
     sends = []
-    order = [lax.rem(c + k, C) for k in list(range(1, C)) + [0]]
+    reach = jnp.minimum(c, C - 1 - c)
+
+    def nearest(n):
+        near = c - (n + 1) // 2 if n % 2 else c + n // 2
+        far = jnp.where(c < C - 1 - c, n, C - 1 - n)
+        return jnp.where(n <= 2 * reach, near, far)
+
+    order = [nearest(n) for n in list(range(C - 1, 0, -1)) + [0]]
 
     def send(src, ssem, rsem, row):
         copy = remote(src, src, ssem, rsem, row, c)
@@ -152,7 +159,7 @@
         part = jnp.dot(a_buf[...], rhs, preferred_element_type=jnp.float32)
         if n < C - 1:
             out_buf[n] = encode(part)
-            copy = remote(out_buf.at[n], in_buf.at[C - 2 - n], zs.at[n], zr.at[C - 2 - n], r, b)
+            copy = remote(out_buf.at[n], in_buf.at[c], zs.at[n], zr.at[c], r, b)
             copy.start()
             sends.append(copy)
         else:
@@ -160,13 +167,12 @@
 
     load_prune.wait()
     for n in range(C - 1):
-        slot = in_buf.at[n]
-        remote(slot, slot, zs.at[n], zr.at[n], r, c).wait_recv()
-        own[...] = own[...] + decode(in_buf[n])
+        other = order[C - 2 - n]
+        arrived(in_buf.at[other], zr.at[other])
+        own[...] = own[...] + decode(in_buf[other])
 
     kept = own[...] * prune_buf[...].astype(jnp.float32)
     inflated = kept * kept
-    infl_out[...] = inflated
     tots[r] = jnp.broadcast_to(
         jnp.sum(inflated, axis=0, keepdims=True), tots.shape[1:]
     )
@@ -183,7 +189,8 @@
     total = tots[0]
     for k in range(1, R):
         total = total + tots[k]
-    tot_out[...] = total / (rows * R) + 1e-05
+    infl_out[...] = inflated / (total / (rows * R) + 1e-05)
+    tot_out[...] = total
 
     for copy in sends:
         copy.wait_send()
@@ -215,7 +222,7 @@
             pltpu.VMEM((rho, C, C, rows // C, cols), bf16),
             pltpu.VMEM((rows, cols), f32),
             pltpu.VMEM((C - 1, rows, cols), jnp.int16),
-            pltpu.VMEM((C - 1, rows, cols), jnp.int16),
+            pltpu.VMEM((C, rows, cols), jnp.int16),
             pltpu.VMEM((R, 1, cols), f32),
             dma((2,)),
             dma((C,)),
@@ -224,13 +231,13 @@
             dma((rho, C, C)),
             dma((C, rho, C)),
             dma((C - 1,)),
-            dma((C - 1,)),
+            dma((C,)),
             dma((R - 1,)),
             dma((R,)),
         ],
         compiler_params=pltpu.CompilerParams(collective_id=0, has_side_effects=True),
     )(matrix, occ_matrix, batch, occ_batch[:, 0], prune_mask)
-    return inflated / total
+    return inflated
 
 
 def body(R, C, matrix, occ_matrix, batch, occ_batch, prune_mask):

time: 33.1 us -> 30.7 us (0.927)
  Pallas kernels: 30.7 us -> 28.9 us
  other arithmetic: 1.62 us -> 0 us
  local copies, waits for them, and re-layouts: 0.6 us -> 1.62 us
    pallas_call x1, Pallas kernels: 30.7 us -> 28.9 us  [kernel_body(): pl.pallas_call(functools.partial(kernel, R, C), out_shape=(jax.ShapeDtype...]
    div x1 -> x0, other arithmetic: 1.62 us -> none  [kernel_body(): return inflated / total]
    unnamed x2 -> x1, local copies, waits for them, and re-layouts: 0.6 us -> 1.62 us
where the time goes in v3:
time: 30.7 us; the launch traced here: 30.6 us
  Pallas kernels  28.9 us (94%)
  local copies, waits for them, and re-layouts  1.62 us (5%)
    pallas_call x1, Pallas kernels, kernel_body(): pl.pallas_call(functools.partial(kernel, R, C), out_shape=(jax.ShapeDtype...  28.9 us
    unnamed x1, local copies, waits for them, and re-layouts  1.62 us

profile of v3, /device:TPU:0, one launch (start us, length us, event | category | flops | bytes accessed | tf_op | source)
XLA Modules:
  0.0 30.6 jit_solution(17168678483769548484)
XLA Ops:
  0.0 28.9 %shard_map.55 = (f32[384,128]{1,0:T(8,128)}, f32[1,128]{1,0:T(1,128)}) custom-call(bf16[384,768]{1,0:T(8,128)(2,1)} %mat_hbm.1, s32[3,6]{1,0:T(4,128)} %occ_m.1, bf16[384,128]{1,0:T(8,128)(2,1)} %bat.1, s32[3]{0:T(128)} %bitcast.1, s32[384,128]{1,0:T(8,128)} %prune_hbm.1), custom_call_target="tpu_custom_call" | custom-call | tf_op jit(solution)/shard_map/pallas_call | solution.py:210
  28.9 1.6 %copy.7 = f32[384,128]{1,0:T(8,128)} copy(f32[384,128]{1,0:T(8,128)} %get-tuple-element.6) | data formatting | bytes 393216
